TPU v7x, 32 devices: a whole 2x2x4 slice. The times are simulated.
32 devices in a mesh: dp: 8 (over y, x, core), fsdp: 4 (over z).
Axes of the slice: x: 2, y: 2, z: 4, core: 2. Of those that a mesh axis runs over, the one named last changes fastest.
Arguments:
- img_emb: bfloat16 [1024, 1024], P(('dp', 'fsdp')), may hold values from -0.25 to 0.25
- txt_emb: bfloat16 [1024, 1024], P(('dp', 'fsdp')), may hold values from -0.25 to 0.25
- img_ids: int32 [1024], P(('dp', 'fsdp')), may hold values from 0 to 1023
- txt_ids: int32 [1024], P(('dp', 'fsdp')), may hold values from 0 to 1023
- temp_log: float32 [1], replicated, may hold values from 1.5 to 2.5
- logit_bias: float32 [1], replicated, may hold values from -6 to -2
- block_in: bfloat16 [2048, 3072], P(('dp', 'fsdp')), may hold values from -6 to 6
- dw_kernel: float32 [49, 3072], replicated, may hold values from -0.875 to 0.875
- ln_gain: float32 [3072], replicated, may hold values from 0.5 to 1.5
- ln_bias: float32 [3072], replicated, may hold values from -3 to 3
- w_up: bfloat16 [3072, 6144], P(None, 'fsdp'), may hold values from -0.109375 to 0.109375
- w_down: bfloat16 [6144, 3072], P('fsdp'), may hold values from -0.078125 to 0.078125
- layer_scale: float32 [3072], replicated, may hold values from 0.1 to 1
- head_gain: float32 [3072], replicated, may hold values from 0.5 to 1.5
- head_bias: float32 [3072], replicated, may hold values from -3 to 3
- w_proj: bfloat16 [3072, 1024], replicated, may hold values from -0.109375 to 0.109375
Outputs:
- img_grad: float32 [1024, 1024], P(('dp', 'fsdp'))
- txt_grad: float32 [1024, 1024], P(('dp', 'fsdp'))
- w_up_grad: float32 [3072, 6144], P('dp', 'fsdp')
- w_down_grad: float32 [6144, 3072], P('fsdp', 'dp')
All inputs are finite; a program needn't handle non-finite values.
Results may differ from a plain program's by a relative error of at most 0.02.
Values may be sent and summed in bfloat16 or wider, within the bound.
A program may use at most 128 MiB of HBM per device.

v0:
```python
import jax
import jax.numpy as jnp
from jax import lax
from jax.sharding import PartitionSpec as P

KERNEL = 7
SIDE = 8


def unit_rows(matrix):
    values = matrix.astype(jnp.float32)
    length = jnp.sqrt(jnp.sum(values * values, axis=1, keepdims=True) + 1e-06)
    return (values / length, length)


def back_unit(gradient, unit_part, length):
    inner_prod = jnp.sum(unit_part * gradient, axis=1, keepdims=True)
    return (gradient - unit_part * inner_prod) / length


def pair_tile(images, image_ids, text_rows, text_ids, temper, offset):
    scores = jnp.dot(images, text_rows.T, preferred_element_type=jnp.float32)
    logits = temper * scores + offset
    labels = jnp.where(image_ids[:, None] == text_ids[None, :], 1.0, -1.0)
    weights = (temper * -labels * jax.nn.sigmoid(-labels * logits)).astype(jnp.bfloat16)
    image_part = jnp.dot(weights, text_rows, preferred_element_type=jnp.float32)
    text_part = jnp.dot(weights.T, images, preferred_element_type=jnp.float32)
    return (image_part, text_part)


def depthwise(pictures, kernel):
    reach = KERNEL // 2
    padded = jnp.pad(pictures, ((0, 0), (reach, reach), (reach, reach), (0, 0)))
    summed = jnp.zeros_like(pictures)
    for above in range(KERNEL):
        for across in range(KERNEL):
            summed = (
                summed
                + kernel[above * KERNEL + across]
                * padded[:, above : above + SIDE, across : across + SIDE, :]
            )
    return summed


def layer_norm(values, gain_vec, bias_vec):
    centre = jnp.mean(values, axis=-1, keepdims=True)
    centred = values - centre
    inverse = 1.0 / jnp.sqrt(jnp.mean(centred * centred, axis=-1, keepdims=True) + 1e-06)
    normal = centred * inverse
    return (normal * gain_vec + bias_vec, normal, inverse)


def head_back(patch_means, block_mean, image_sum, layer_scale, head_gain, head_bias, w_proj):
    pooled = patch_means.astype(jnp.float32) + layer_scale * block_mean
    head_out, head_norm, inverse = layer_norm(pooled, head_gain, head_bias)
    embed = jnp.dot(head_out.astype(jnp.bfloat16), w_proj, preferred_element_type=jnp.float32)
    embed_unit, embed_len = unit_rows(embed)
    embed_grad = back_unit(image_sum, embed_unit, embed_len).astype(jnp.bfloat16)
    head_grad = jnp.dot(embed_grad, w_proj.T, preferred_element_type=jnp.float32)
    norm_grad = head_grad * head_gain
    pool_grad = inverse * (
        norm_grad
        - jnp.mean(norm_grad, axis=1, keepdims=True)
        - head_norm * jnp.mean(norm_grad * head_norm, axis=1, keepdims=True)
    )
    return (layer_scale * pool_grad / (SIDE * SIDE)).astype(jnp.bfloat16)


def on_device(
    img_emb,
    txt_emb,
    img_ids,
    txt_ids,
    temp_log,
    logit_bias,
    block_in,
    dw_kernel,
    ln_gain,
    ln_bias,
    w_up,
    w_down,
    layer_scale,
    head_gain,
    head_bias,
    w_proj,
):
    channels = block_in.shape[1]
    hid_width = w_up.shape[1]
    temper = jnp.exp(temp_log[0])
    offset = logit_bias[0]
    img_unit, img_len = unit_rows(img_emb)
    txt_unit, txt_len = unit_rows(txt_emb)
    img_b = img_unit.astype(jnp.bfloat16)
    txt_b = txt_unit.astype(jnp.bfloat16)
    pictures = block_in.astype(jnp.float32).reshape(1, SIDE, SIDE, channels)
    mixed_rows = depthwise(pictures, dw_kernel).reshape(SIDE * SIDE, channels)
    normed = layer_norm(mixed_rows, ln_gain, ln_bias)[0].astype(jnp.bfloat16)
    patch_means = jnp.mean(pictures, axis=(1, 2)).astype(jnp.bfloat16)
    group_img, group_ids, group_normed = (
        lax.all_gather(img_b, "fsdp", axis=0, tiled=True),
        lax.all_gather(img_ids, "fsdp", axis=0, tiled=True),
        lax.all_gather(normed, "fsdp", axis=0, tiled=True),
    )
    image_count = group_normed.shape[0] // (SIDE * SIDE)
    image_part, text_part = pair_tile(
        group_img,
        group_ids,
        lax.all_gather(txt_b, "dp", axis=0, tiled=True),
        lax.all_gather(txt_ids, "dp", axis=0, tiled=True),
        temper,
        offset,
    )
    image_acc = image_part
    image_acc = lax.optimization_barrier(image_acc.astype(jnp.bfloat16)).astype(jnp.float32)
    hidden = jnp.dot(group_normed, w_up, preferred_element_type=jnp.float32)
    active = jax.nn.gelu(hidden).astype(jnp.bfloat16)
    active_total = jnp.sum(
        active.astype(jnp.float32).reshape(image_count, SIDE * SIDE, hid_width), axis=1
    )
    down_wide = w_down.astype(jnp.float32)
    partial_mean = jnp.dot(active_total / (SIDE * SIDE), down_wide, precision=lax.Precision.HIGHEST)
    image_sum, block_mean = (
        lax.psum_scatter(
            image_acc.astype(jnp.bfloat16), "fsdp", scatter_dimension=0, tiled=True
        ).astype(jnp.float32),
        lax.psum_scatter(
            partial_mean.astype(jnp.bfloat16), "fsdp", scatter_dimension=0, tiled=True
        ).astype(jnp.float32),
    )
    grad_row = head_back(
        patch_means, block_mean, image_sum[:1], layer_scale, head_gain, head_bias, w_proj
    )
    group_grad = lax.all_gather(grad_row, "fsdp", axis=0, tiled=True)
    row_down = jnp.dot(group_grad, w_down.T, preferred_element_type=jnp.float32)
    down_grad = jnp.broadcast_to(
        row_down[:, None, :], (image_count, SIDE * SIDE, hid_width)
    ).reshape(-1, hid_width)
    _, pullback = jax.vjp(jax.nn.gelu, hidden)
    hid_grad = pullback(down_grad)[0].astype(jnp.bfloat16)
    down_part = jnp.dot(
        active_total.T, group_grad.astype(jnp.float32), precision=lax.Precision.HIGHEST
    )
    up_part = jnp.dot(group_normed.T, hid_grad, preferred_element_type=jnp.float32)
    w_up_grad, w_down_grad, text_sum = (
        lax.psum_scatter(
            up_part.astype(jnp.bfloat16), "dp", scatter_dimension=0, tiled=True
        ).astype(jnp.float32),
        lax.psum_scatter(
            down_part.astype(jnp.bfloat16), "dp", scatter_dimension=1, tiled=True
        ).astype(jnp.float32),
        lax.psum_scatter(
            text_part.astype(jnp.bfloat16), "dp", scatter_dimension=0, tiled=True
        ).astype(jnp.float32),
    )
    img_grad = back_unit(image_sum, img_unit, img_len)
    txt_grad = back_unit(text_sum, txt_unit, txt_len)
    return (img_grad, txt_grad, w_up_grad, w_down_grad)


def solution(mesh):
    in_specs = (
        P(("dp", "fsdp"), None),
        P(("dp", "fsdp"), None),
        P(("dp", "fsdp")),
        P(("dp", "fsdp")),
        P(),
        P(),
        P(("dp", "fsdp"), None),
        P(),
        P(),
        P(),
        P(None, "fsdp"),
        P("fsdp", None),
        P(),
        P(),
        P(),
        P(),
    )
    out_specs = (P(("dp", "fsdp"), None), P(("dp", "fsdp"), None), P("dp", "fsdp"), P("fsdp", "dp"))
    return jax.shard_map(
        on_device, mesh=mesh, in_specs=in_specs, out_specs=out_specs, check_vma=False
    )
```

profile of v0, /device:TPU:0, one launch (start us, length us, event | category | flops | bytes accessed | tf_op | source)
XLA Modules:
  0.0 363.6 jit_solution(8530367770583388540)
XLA Ops:
  10.4 1.4 fusion.155
  15.3 9.9 %all-reduce.1 = s32[128]{0:T(128)S(1)} all-reduce(s32[128]{0:T(128)S(1)} %dynamic-update-slice), channel_id=1, replica_groups=mesh['dp'=8,'fsdp'=4] {'fsdp'}, use_global_device_ids=true, to_apply=%add.1 | all-reduce | flops 128 | bytes 1024
  26.1 8.0 %all-reduce.2 = s32[256]{0:T(256)S(1)} all-reduce(s32[256]{0:T(256)S(1)} %dynamic-update-slice.1), channel_id=1, replica_groups=mesh['dp'=8,'fsdp'=4] {'dp'}, use_global_device_ids=true, to_apply=%add.2 | all-reduce | flops 256 | bytes 2048
  35.9 14.2 %all_gather.20 = bf16[128,1024]{1,0:T(8,128)(2,1)S(1)} all-gather(bf16[32,1024]{1,0:T(8,128)(2,1)S(1)} %fusion.145), channel_id=1, replica_groups=mesh['dp'=8,'fsdp'=4] {'fsdp'}, dimensions={0}, use_global_device_ids=true | all-gather | bytes 327680 | tf_op jit(solution)/shard_map/all_gather | solution.py:100
  50.2 9.0 %all_gather.21 = bf16[256,1024]{1,0:T(8,128)(2,1)S(1)} all-gather(bf16[32,1024]{1,0:T(8,128)(2,1)S(1)} %fusion.146), channel_id=1, replica_groups=mesh['dp'=8,'fsdp'=4] {'dp'}, dimensions={0}, use_global_device_ids=true | all-gather | bytes 589824 | tf_op jit(solution)/shard_map/all_gather | solution.py:108
  61.1 5.5 %fusion.150 = (f32[8,8]{1,0:T(8,128)S(1)}, f32[1,8,8,3072]{3,2,1,0:T(8,128)S(1)}) fusion(f32[3072]{0:T(1024)S(1)} %bitcast.138, f32[3072]{0:T(1024)S(1)} %bitcast.139, f32[3072]{0:T(1024)S(1)} %bitcast.142, f32[3072]{0:T(1024)S(1)} %bitcast.143, f32[3072]{0:T(1024)S(1)} %bitcast.144, f32[3072]{0:T(1024)S(1)} %bitcast.145, f32[3072]{0:T(1024)S(1)} %bitcast.146, ...), kind=kLoop, calls=%fused_computation.236 | loop fusion | flops 19267520 | bytes 2175232 | tf_op jit(solution)/shard_map/reduce_sum | solution.py:46
  69.3 10.2 %reduce-scatter.7.cloned.1.call-done = bf16[32,1024]{1,0:T(8,128)(2,1)} async-done(((bf16[128,1024]{1,0:T(8,128)(2,1)}), bf16[32,1024]{1,0:T(8,128)(2,1)}) %reduce-scatter.7.cloned.1.call-update) | async-done | bytes 65552 | tf_op jit(solution)/shard_map/reduce_scatter | solution.py:123
  80.4 36.6 %all-gather.3.cloned.1.call-done = bf16[256,3072]{1,0:T(8,128)(2,1)} async-done(((bf16[64,3072]{1,0:T(8,128)(2,1)}), bf16[256,3072]{1,0:T(8,128)(2,1)}) %all-gather.3.cloned.1.call-update) | async-done | bytes 1572880 | tf_op jit(solution)/shard_map/all_gather | solution.py:102
  117.0 5.9 %convert_reduce_fusion = (f32[4,1536]{1,0:T(4,128)S(1)}, f32[256,1536]{1,0:T(8,128)S(1)}) fusion(bf16[256,3072]{1,0:T(8,128)(2,1)} %all-gather.3.cloned.1.call-done, bf16[3072,1536]{1,0:T(8,128)(2,1)} %param.26), kind=kOutput, calls=%fused_computation.65 | convolution fusion | flops 2420238336 | bytes 12607488 | tf_op jit(solution)/shard_map/dot_general | solution.py:115
  122.9 6.3 %convolution_convert_fusion.2 = bf16[4,3072]{1,0:T(4,128)(2,1)S(1)} fusion(bf16[1536,3072]{1,0:T(8,128)(2,1)} %param.27, f32[4,1536]{1,0:T(4,128)S(1)} %get-tuple-element.61), kind=kOutput, calls=%fused_computation.50 | convolution fusion | flops 226510848 | bytes 9486336 | tf_op jit(solution)/shard_map/dot_general | solution.py:121
  129.2 16.9 %all-reduce.3 = bf16[4,3072]{1,0:T(4,128)(2,1)S(1)} all-reduce(bf16[4,3072]{1,0:T(4,128)(2,1)S(1)} %convolution_convert_fusion.2), channel_id=4, replica_groups=mesh['dp'=8,'fsdp'=4] {'fsdp'}, use_global_device_ids=true, to_apply=%region_10.11.clone | all-reduce | flops 12288 | bytes 49152
  149.4 3.7 %fusion.126 = f32[1,1024]{1,0:T(1,128)S(1)} fusion(bf16[3072,1024]{1,0:T(8,128)(2,1)} %param.31, f32[1,3072]{1,0:T(1,128)S(1)} %bitcast.186, f32[1,3072]{1,0:T(1,128)S(1)} %bitcast.183, f32[1,3072]{1,0:T(1,128)S(1)} %get-tuple-element.7, f32[]{:T(128)S(6)} %sqrt.32, f32[]{:T(128)S(6)} %div.98), kind=kOutput, calls=%fused_computation.198 | convolution fusion | flops 6306816 | bytes 6332424 | tf_op jit(solution)/shard_map/dot_general | solution.py:56
  155.7 4.5 %fusion.137 = f32[1,3072]{1,0:T(1,128)S(1)} fusion(bf16[3072,1024]{1,0:T(8,128)(2,1)} %param.31, f32[1,1024]{1,0:T(1,128)S(1)} %bitcast.184, f32[32,1024]{1,0:T(8,128)S(1)} %convert_element_type.105, f32[]{:T(128)S(6)} %sqrt.33), kind=kOutput, calls=%fused_computation.216 | convolution fusion | flops 6294528 | bytes 6311940 | tf_op jit(solution)/shard_map/dot_general | solution.py:59
  162.8 13.3 %all-gather = bf16[4,1,3072]{2,1,0:T(2,128)(2,1)S(1)} all-gather(bf16[1,1,3072]{2,1,0:T(2,128)(2,1)S(1)} %convert_bitcast_fusion.1), channel_id=1, replica_groups=mesh['dp'=8,'fsdp'=4] {'fsdp'}, dimensions={0}, use_global_device_ids=true | all-gather | bytes 30720 | tf_op jit(solution)/shard_map/all_gather | solution.py:133
  176.1 9.7 %convolution_convert_fusion = bf16[1536,3072]{1,0:T(8,128)(2,1)} fusion(f32[4,1536]{1,0:T(4,128)S(1)} %get-tuple-element.61, bf16[4,1,3072]{2,1,0:T(2,128)(2,1)S(1)} %all-gather), kind=kOutput, calls=%fused_computation.48 | convolution fusion | flops 231211008 | bytes 9486336 | tf_op jit(solution)/shard_map/dot_general | solution.py:140
  185.8 12.7 %copy.20 = bf16[1536,3072]{0,1:T(8,128)(2,1)} copy(bf16[1536,3072]{1,0:T(8,128)(2,1)} %convolution_convert_fusion) | data formatting | bytes 18874368
  198.6 6.2 %fusion.123 = f32[4,1536]{1,0:T(4,128)S(1)} fusion(bf16[1536,3072]{1,0:T(8,128)(2,1)} %param.27, bf16[4,1,3072]{2,1,0:T(2,128)(2,1)S(1)} %all-gather), kind=kOutput, calls=%fused_computation.195 | convolution fusion | flops 37748736 | bytes 9486336 | tf_op jit(solution)/shard_map/dot_general | solution.py:134
  206.6 6.4 %convolution_convert_fusion.1 = bf16[3072,1536]{1,0:T(8,128)(2,1)} fusion(bf16[256,3072]{1,0:T(8,128)(2,1)S(1)} %copy-done, bf16[256,1536]{1,0:T(8,128)(2,1)S(1)} %fusion.6), kind=kOutput, calls=%fused_computation.49 | convolution fusion | flops 2420637696 | bytes 11796480 | tf_op jit(solution)/shard_map/dot_general | solution.py:143
  215.8 1.6 fusion.121
  217.4 56.5 %reduce-scatter.13.cloned.1.call-done = bf16[384,1536]{1,0:T(8,128)(2,1)} async-done(((bf16[3072,1536]{1,0:T(8,128)(2,1)}), bf16[384,1536]{1,0:T(8,128)(2,1)}) %reduce-scatter.13.cloned.1.call-update) | async-done | bytes 1179664
  273.9 1.7 copy.21
  275.6 1.6 convert_element_type.123
  277.2 76.9 %reduce-scatter.11.cloned.1.call-done = bf16[384,1536]{1,0:T(8,128)(2,1)} async-done(((bf16[3072,1536]{1,0:T(8,128)(2,1)}), bf16[384,1536]{1,0:T(8,128)(2,1)}) %reduce-scatter.11.cloned.1.call-update) | async-done | bytes 1179664 | tf_op jit(solution)/shard_map/reduce_scatter | solution.py:145
  354.1 3.0 convert_element_type.121
  (74 shorter events, 22.0 us)
Async XLA Ops:
  7.2 72.4 %reduce-scatter.7.cloned.1.call-start = ((), (), s32[]{:S(2)}) async-start(), calls=%async_computation.4 | async-start | bytes 327680 | tf_op jit(solution)/shard_map/reduce_scatter | solution.py:123
  50.2 10.3 %copy-start.5 = (f32[49,3072]{1,0:T(8,128)S(1)}, f32[49,3072]{1,0:T(8,128)}, u32[]{:S(2)}) copy-start(f32[49,3072]{1,0:T(8,128)} %param.23) | copy-start | bytes 1806340
  59.2 1.8 copy-start.1
  60.5 56.5 %all-gather.3.cloned.1.call-start = ((), (), s32[]{:S(2)}) async-start(), calls=%async_computation.6 | async-start | bytes 1966080 | tf_op jit(solution)/shard_map/all_gather | solution.py:102
  61.0 6.0 %copy-start.8 = (f32[3072]{0:T(1024)S(1)}, f32[3072]{0:T(1024)}, u32[]{:S(2)}) copy-start(f32[3072]{0:T(1024)} %param.25) | copy-start | bytes 36868
  61.1 5.9 %copy-start.9 = (f32[3072]{0:T(1024)S(1)}, f32[3072]{0:T(1024)}, u32[]{:S(2)}) copy-start(f32[3072]{0:T(1024)} %param.24) | copy-start | bytes 36868
  68.0 146.8 %reduce-scatter.9.cloned.1.call-start = ((), (), s32[]{:S(2)}) async-start(), calls=%async_computation.5 | async-start | bytes 589824 | tf_op jit(solution)/shard_map/reduce_scatter | solution.py:151
  69.2 204.7 %reduce-scatter.13.cloned.1.call-start = ((), (), s32[]{:S(2)}) async-start(), calls=%async_computation.8 | async-start | bytes 10616832
  122.9 23.2 %copy-start.6 = (f32[3072]{0:T(1024)S(1)}, f32[3072]{0:T(1024)}, u32[]{:S(2)}) copy-start(f32[3072]{0:T(1024)} %param.28) | copy-start | bytes 36868
  122.9 26.5 %copy-start.7 = (f32[3072]{0:T(1024)S(1)}, f32[3072]{0:T(1024)}, u32[]{:S(2)}) copy-start(f32[3072]{0:T(1024)} %param.29) | copy-start | bytes 36868
  122.9 26.5 %copy-start.10 = (f32[3072]{0:T(1024)S(1)}, f32[3072]{0:T(1024)}, u32[]{:S(2)}) copy-start(f32[3072]{0:T(1024)} %param.30) | copy-start | bytes 36868
  198.5 155.6 %reduce-scatter.11.cloned.1.call-start = ((), (), s32[]{:S(2)}) async-start(), calls=%async_computation.7 | async-start | bytes 10616832 | tf_op jit(solution)/shard_map/reduce_scatter | solution.py:145
  204.8 1.8 copy-start
  212.9 0.8 copy-start.2
  212.9 0.9 copy-start.4
  212.9 1.8 copy-start.3
Sparse Core Ops, SparseCore 0:
  60.6 18.9 reduce-scatter.6
  81.7 35.2 all-gather.2
  120.7 32.9 reduce-scatter.8
  198.6 75.2 reduce-scatter.12
  277.3 76.8 reduce-scatter.10
where the time goes:
time: 365 us; the launch traced here: 364 us
  waiting for transfers between devices  180 us (49%)
  blocking collectives  71.3 us (20%)
  matrix products  45.1 us (12%)
  other arithmetic  25.8 us (7%)
  local copies, waits for them, and re-layouts  20.9 us (6%)
  between operations  20 us (5%)
    reduce_scatter x1, waiting for transfers between devices, on_device(): lax.psum_scatter(up_part.astype(jnp.bfloat16), 'dp', scatter_dimension=0,...  76.9 us
    unnamed x6, waiting for transfers between devices  56.6 us
    all_gather x1, waiting for transfers between devices, on_device(): lax.all_gather(normed, 'fsdp', axis=0, tiled=True)  36.6 us
    unnamed x3, blocking collectives  34.8 us
    unnamed x30, local copies, waits for them, and re-layouts  20.4 us
    all_gather x1, blocking collectives, on_device(): lax.all_gather(img_b, 'fsdp', axis=0, tiled=True)  14.2 us
    all_gather x1, blocking collectives, on_device(): group_grad = lax.all_gather(grad_row, 'fsdp', axis=0, tiled=True)  13.3 us
    reduce_scatter x1, waiting for transfers between devices, on_device(): lax.psum_scatter(image_acc.astype(jnp.bfloat16), 'fsdp', scatter_dimensio...  10.2 us
  transfers between devices with their start and end apart: 5, of which 4 were waited for; matrix products, arithmetic and copies ran while one was open for 21% of the time, Pallas kernels for 0%

commit v1 on v0

--- a/solution.py
+++ b/solution.py
@@ -5,6 +5,28 @@
 
 KERNEL = 7
 SIDE = 8
+
+
+def joined_along(tiles, dim):
+    shape = list(tiles.shape[1:])
+    shape[dim] *= tiles.shape[0]
+    return jnp.moveaxis(tiles, 0, dim).reshape(shape)
+
+
+def gather_around(x, axis, dim):
+    devices = lax.axis_size(axis)
+    pairs = [(i, (i + 1) % devices) for i in range(devices)]
+    back = [(b, a) for a, b in pairs]
+    lower, upper = ([], [])
+    for turn in range(devices - 1):
+        if turn % 2 == 0:
+            lower.append(lax.ppermute(lower[-1] if lower else x, axis, pairs))
+        else:
+            upper.append(lax.ppermute(upper[-1] if upper else x, axis, back))
+    blocks = jnp.stack([*lower[::-1], x, *upper])
+    shift = lax.axis_index(axis) - len(lower)
+    blocks = blocks[(jnp.arange(devices) - shift) % devices]
+    return joined_along(blocks, dim)
 
 
 def unit_rows(matrix):
@@ -99,7 +121,7 @@
     group_img, group_ids, group_normed = (
         lax.all_gather(img_b, "fsdp", axis=0, tiled=True),
         lax.all_gather(img_ids, "fsdp", axis=0, tiled=True),
-        lax.all_gather(normed, "fsdp", axis=0, tiled=True),
+        gather_around(normed, "fsdp", 0),
     )
     image_count = group_normed.shape[0] // (SIDE * SIDE)
     image_part, text_part = pair_tile(

time: 365 us -> 354 us (0.970)
  waiting for transfers between devices: 180 us -> 165 us
  starting transfers between devices: 0.2 us -> 4.03 us
    all_gather x1 -> x0, waiting for transfers between devices: 36.6 us -> none  [on_device(): lax.all_gather(normed, 'fsdp', axis=0, tiled=True)]
    ppermute x0 -> x3, waiting for transfers between devices: none -> 29.5 us  [the longest x2 29.5 us: gather_around(): lower.append(lax.ppermute(lower[-1] if lower else x, axis, pairs))]
    reduce_scatter x1, waiting for transfers between devices: 10.2 us -> 0.02 us  [on_device(): lax.psum_scatter(image_acc.astype(jnp.bfloat16), 'fsdp', scatter_dimensio...]
    ppermute x0 -> x3, starting transfers between devices: none -> 3.86 us  [the longest x1 2.3 us: gather_around(): upper.append(lax.ppermute(upper[-1] if upper else x, axis, back))]
    unnamed x6 -> x5, waiting for transfers between devices: 56.6 us -> 58.2 us
    unnamed x30 -> x36, local copies, waits for them, and re-layouts: 20.4 us -> 19.7 us
  transfers between devices with their start and end apart: 5 -> 7, of which waited for: 4 -> 4; matrix products, arithmetic and copies ran while one was open for 21% -> 23% of each run, Pallas kernels for 0% -> 0%
where the time goes in v1:
time: 354 us; the launch traced here: 353 us
  waiting for transfers between devices  165 us (47%)
  blocking collectives  70.2 us (20%)
  matrix products  44.8 us (13%)
  other arithmetic  26.6 us (8%)
  local copies, waits for them, and re-layouts  22.4 us (6%)
  between operations  20.1 us (6%)
  starting transfers between devices  4.03 us (1%)
    reduce_scatter x1, waiting for transfers between devices, on_device(): lax.psum_scatter(up_part.astype(jnp.bfloat16), 'dp', scatter_dimension=0,...  76.9 us
    unnamed x5, waiting for transfers between devices  58.2 us
    unnamed x3, blocking collectives  33.9 us
    ppermute x2, waiting for transfers between devices, gather_around(): lower.append(lax.ppermute(lower[-1] if lower else x, axis, pairs))  29.5 us
    unnamed x36, local copies, waits for them, and re-layouts  19.7 us
    all_gather x1, blocking collectives, on_device(): lax.all_gather(img_b, 'fsdp', axis=0, tiled=True)  14.2 us
    all_gather x1, blocking collectives, on_device(): group_grad = lax.all_gather(grad_row, 'fsdp', axis=0, tiled=True)  13.1 us
    dot_general x1, matrix products, on_device(): jnp.dot(active_total.T, group_grad.astype(jnp.float32), precision=lax.Pre...  9.72 us
  transfers between devices with their start and end apart: 7, of which 4 were waited for; matrix products, arithmetic and copies ran while one was open for 23% of the time, Pallas kernels for 0%

profile of v1, /device:TPU:0, one launch (start us, length us, event | category | flops | bytes accessed | tf_op | source)
XLA Modules:
  0.0 352.7 jit_solution(15808672135546497126)
XLA Ops:
  15.3 9.9 %all-reduce.1 = s32[128]{0:T(128)S(1)} all-reduce(s32[128]{0:T(128)S(1)} %dynamic-update-slice), channel_id=1, replica_groups=mesh['dp'=8,'fsdp'=4] {'fsdp'}, use_global_device_ids=true, to_apply=%add.1 | all-reduce | flops 128 | bytes 1024
  26.1 8.0 %all-reduce.2 = s32[256]{0:T(256)S(1)} all-reduce(s32[256]{0:T(256)S(1)} %dynamic-update-slice.1), channel_id=1, replica_groups=mesh['dp'=8,'fsdp'=4] {'dp'}, use_global_device_ids=true, to_apply=%add.2 | all-reduce | flops 256 | bytes 2048
  35.9 14.2 %all_gather.17 = bf16[128,1024]{1,0:T(8,128)(2,1)S(1)} all-gather(bf16[32,1024]{1,0:T(8,128)(2,1)S(1)} %fusion.151), channel_id=1, replica_groups=mesh['dp'=8,'fsdp'=4] {'fsdp'}, dimensions={0}, use_global_device_ids=true | all-gather | bytes 327680 | tf_op jit(solution)/shard_map/all_gather | solution.py:122
  50.2 9.0 %all_gather.18 = bf16[256,1024]{1,0:T(8,128)(2,1)S(1)} all-gather(bf16[32,1024]{1,0:T(8,128)(2,1)S(1)} %fusion.152), channel_id=1, replica_groups=mesh['dp'=8,'fsdp'=4] {'dp'}, dimensions={0}, use_global_device_ids=true | all-gather | bytes 589824 | tf_op jit(solution)/shard_map/all_gather | solution.py:130
  61.1 5.5 %fusion.156 = (f32[8,8]{1,0:T(8,128)S(1)}, f32[1,8,8,3072]{3,2,1,0:T(8,128)S(1)}) fusion(f32[3072]{0:T(1024)S(1)} %bitcast.161, f32[3072]{0:T(1024)S(1)} %bitcast.162, f32[3072]{0:T(1024)S(1)} %bitcast.165, f32[3072]{0:T(1024)S(1)} %bitcast.166, f32[3072]{0:T(1024)S(1)} %bitcast.167, f32[3072]{0:T(1024)S(1)} %bitcast.168, f32[3072]{0:T(1024)S(1)} %bitcast.169, ...), kind=kLoop, calls=%fused_computation.250 | loop fusion | flops 19267520 | bytes 2175232 | tf_op jit(solution)/shard_map/reduce_sum | solution.py:68
  67.2 2.3 collective-permute-start.2
  70.9 19.5 %collective-permute-done = bf16[64,3072]{1,0:T(8,128)(2,1)S(1)} collective-permute-done((bf16[64,3072]{1,0:T(8,128)(2,1)S(1)}, bf16[64,3072]{1,0:T(8,128)(2,1)S(1)}, u32[]{:S(2)}, u32[]{:S(2)}) %collective-permute-start) | collective-permute-done | bytes 393248 | tf_op jit(solution)/shard_map/ppermute | solution.py:23
  92.9 10.0 %collective-permute-done.1 = bf16[64,3072]{1,0:T(8,128)(2,1)S(1)} collective-permute-done((bf16[64,3072]{1,0:T(8,128)(2,1)S(1)}, bf16[64,3072]{1,0:T(8,128)(2,1)S(1)}, u32[]{:S(2)}, u32[]{:S(2)}) %collective-permute-start.1) | collective-permute-done | bytes 393248 | tf_op jit(solution)/shard_map/ppermute | solution.py:23
  104.3 2.1 gather_fusion
  106.5 7.8 %convert_reduce_fusion = (f32[4,1536]{1,0:T(4,128)S(1)}, f32[256,1536]{1,0:T(8,128)}) fusion(bf16[256,3072]{1,0:T(8,128)(2,1)S(1)} %bitcast.142, bf16[3072,1536]{1,0:T(8,128)(2,1)} %param.26), kind=kOutput, calls=%fused_computation.67 | convolution fusion | flops 2420238336 | bytes 12607488 | tf_op jit(solution)/shard_map/dot_general | solution.py:137
  114.4 3.8 %convolution_convert_fusion.2 = bf16[4,3072]{1,0:T(4,128)(2,1)S(1)} fusion(bf16[1536,3072]{1,0:T(8,128)(2,1)S(1)} %bitcast.140, f32[4,1536]{1,0:T(4,128)S(1)} %get-tuple-element.61), kind=kOutput, calls=%fused_computation.51 | convolution fusion | flops 226510848 | bytes 9486336 | tf_op jit(solution)/shard_map/dot_general | solution.py:143
  118.2 15.9 %all-reduce.3 = bf16[4,3072]{1,0:T(4,128)(2,1)S(1)} all-reduce(bf16[4,3072]{1,0:T(4,128)(2,1)S(1)} %convolution_convert_fusion.2), channel_id=4, replica_groups=mesh['dp'=8,'fsdp'=4] {'fsdp'}, use_global_device_ids=true, to_apply=%region_10.11.clone | all-reduce | flops 12288 | bytes 49152
  137.4 3.7 %fusion.130 = f32[1,1024]{1,0:T(1,128)S(1)} fusion(bf16[3072,1024]{1,0:T(8,128)(2,1)} %param.31, f32[1,3072]{1,0:T(1,128)S(1)} %bitcast.209, f32[1,3072]{1,0:T(1,128)S(1)} %bitcast.206, f32[1,3072]{1,0:T(1,128)S(1)} %get-tuple-element.7, f32[]{:T(128)S(6)} %sqrt.32, f32[]{:T(128)S(6)} %div.98), kind=kOutput, calls=%fused_computation.205 | convolution fusion | flops 6306816 | bytes 6332424 | tf_op jit(solution)/shard_map/dot_general | solution.py:78
  143.7 4.5 %fusion.141 = f32[1,3072]{1,0:T(1,128)S(1)} fusion(bf16[3072,1024]{1,0:T(8,128)(2,1)} %param.31, f32[1,1024]{1,0:T(1,128)S(1)} %bitcast.207, f32[32,1024]{1,0:T(8,128)S(1)} %convert_element_type.114, f32[]{:T(128)S(6)} %sqrt.33), kind=kOutput, calls=%fused_computation.224 | convolution fusion | flops 6294528 | bytes 6311940 | tf_op jit(solution)/shard_map/dot_general | solution.py:81
  150.8 13.1 %all-gather = bf16[4,1,3072]{2,1,0:T(2,128)(2,1)S(1)} all-gather(bf16[1,1,3072]{2,1,0:T(2,128)(2,1)S(1)} %convert_bitcast_fusion.1), channel_id=1, replica_groups=mesh['dp'=8,'fsdp'=4] {'fsdp'}, dimensions={0}, use_global_device_ids=true | all-gather | bytes 30720 | tf_op jit(solution)/shard_map/all_gather | solution.py:155
  163.9 9.7 %convolution_convert_fusion = bf16[1536,3072]{1,0:T(8,128)(2,1)} fusion(f32[4,1536]{1,0:T(4,128)S(1)} %get-tuple-element.61, bf16[4,1,3072]{2,1,0:T(2,128)(2,1)S(1)} %all-gather), kind=kOutput, calls=%fused_computation.49 | convolution fusion | flops 231211008 | bytes 9486336 | tf_op jit(solution)/shard_map/dot_general | solution.py:162
  173.6 12.7 %copy.20 = bf16[1536,3072]{0,1:T(8,128)(2,1)} copy(bf16[1536,3072]{1,0:T(8,128)(2,1)} %convolution_convert_fusion) | data formatting | bytes 18874368
  186.4 6.3 %fusion.127 = f32[4,1536]{1,0:T(4,128)S(1)} fusion(bf16[1536,3072]{1,0:T(8,128)(2,1)} %param.27, bf16[4,1,3072]{2,1,0:T(2,128)(2,1)S(1)} %all-gather), kind=kOutput, calls=%fused_computation.202 | convolution fusion | flops 37748736 | bytes 9486336 | tf_op jit(solution)/shard_map/dot_general | solution.py:156
  193.8 6.5 %convolution_convert_fusion.1 = bf16[3072,1536]{1,0:T(8,128)(2,1)} fusion(bf16[256,3072]{1,0:T(8,128)(2,1)S(1)} %bitcast.143, bf16[256,1536]{1,0:T(8,128)(2,1)S(1)} %fusion.6), kind=kOutput, calls=%fused_computation.50 | convolution fusion | flops 2420637696 | bytes 11796480 | tf_op jit(solution)/shard_map/dot_general | solution.py:165
  203.3 1.6 fusion.125
  204.9 58.1 %reduce-scatter.13.cloned.1.call-done = bf16[384,1536]{1,0:T(8,128)(2,1)} async-done(((bf16[3072,1536]{1,0:T(8,128)(2,1)}), bf16[384,1536]{1,0:T(8,128)(2,1)}) %reduce-scatter.13.cloned.1.call-update) | async-done | bytes 1179664
  263.0 1.7 copy.21
  266.3 76.9 %reduce-scatter.11.cloned.1.call-done = bf16[384,1536]{1,0:T(8,128)(2,1)} async-done(((bf16[3072,1536]{1,0:T(8,128)(2,1)}), bf16[384,1536]{1,0:T(8,128)(2,1)}) %reduce-scatter.11.cloned.1.call-update) | async-done | bytes 1179664 | tf_op jit(solution)/shard_map/reduce_scatter | solution.py:167
  343.2 3.0 convert_element_type.131
  (89 shorter events, 26.6 us)
Async XLA Ops:
  7.2 84.9 %reduce-scatter.7.cloned.1.call-start = ((), (), s32[]{:S(2)}) async-start(), calls=%async_computation.4 | async-start | bytes 327680 | tf_op jit(solution)/shard_map/reduce_scatter | solution.py:145
  50.2 10.4 %copy-start.5 = (f32[49,3072]{1,0:T(8,128)S(1)}, f32[49,3072]{1,0:T(8,128)}, u32[]{:S(2)}) copy-start(f32[49,3072]{1,0:T(8,128)} %param.23) | copy-start | bytes 1806340
  59.2 1.8 copy-start.1
  60.5 141.7 %reduce-scatter.9.cloned.1.call-start = ((), (), s32[]{:S(2)}) async-start(), calls=%async_computation.5 | async-start | bytes 589824 | tf_op jit(solution)/shard_map/reduce_scatter | solution.py:173
  61.1 6.0 %copy-start.6 = (f32[3072]{0:T(1024)S(1)}, f32[3072]{0:T(1024)}, u32[]{:S(2)}) copy-start(f32[3072]{0:T(1024)} %param.25) | copy-start | bytes 36868
  61.1 6.0 %copy-start.7 = (f32[3072]{0:T(1024)S(1)}, f32[3072]{0:T(1024)}, u32[]{:S(2)}) copy-start(f32[3072]{0:T(1024)} %param.24) | copy-start | bytes 36868
  67.2 25.7 %collective-permute-start.2 = (bf16[64,3072]{1,0:T(8,128)(2,1)S(1)}, bf16[64,3072]{1,0:T(8,128)(2,1)S(1)}, u32[]{:S(2)}, u32[]{:S(2)}) collective-permute-start(bf16[64,3072]{1,0:T(8,128)(2,1)S(1)} %fusion.121), channel_id=1, source_target_pairs={{1,0},{2,1},{3,2},{0,3},{5,4},{6,5},{7,6},{4,7},{9,8},{10,9},{11,1... | collective-permute-start | bytes 1179656 | tf_op jit(solution)/shard_map/ppermute | solution.py:25
  69.5 20.9 %collective-permute-start = (bf16[64,3072]{1,0:T(8,128)(2,1)S(1)}, bf16[64,3072]{1,0:T(8,128)(2,1)S(1)}, u32[]{:S(2)}, u32[]{:S(2)}) collective-permute-start(bf16[64,3072]{1,0:T(8,128)(2,1)S(1)} %fusion.121), channel_id=1, source_target_pairs={{0,1},{1,2},{2,3},{3,0},{4,5},{5,6},{6,7},{7,4},{8,9},{9,10},{10,1... | collective-permute-start | bytes 1179656 | tf_op jit(solution)/shard_map/ppermute | solution.py:23
  70.7 192.3 %reduce-scatter.13.cloned.1.call-start = ((), (), s32[]{:S(2)}) async-start(), calls=%async_computation.7 | async-start | bytes 10616832
  90.4 12.6 %collective-permute-start.1 = (bf16[64,3072]{1,0:T(8,128)(2,1)S(1)}, bf16[64,3072]{1,0:T(8,128)(2,1)S(1)}, u32[]{:S(2)}, u32[]{:S(2)}) collective-permute-start(bf16[64,3072]{1,0:T(8,128)(2,1)S(1)} %collective-permute-done), channel_id=1, source_target_pairs={{0,1},{1,2},{2,3},{3,0},{4,5},{5,6},{6,7},{7,4},{8,9},{9,10},{10,1... | collective-permute-start | bytes 1179656 | tf_op jit(solution)/shard_map/ppermute | solution.py:23
  104.3 10.0 %slice-start = ((s8[9437184]{0:T(1024)(128)(4,1)}), s8[1048576]{0:T(1024)(128)(4,1)S(1)}, s32[]{:S(2)}) async-start(s8[9437184]{0:T(1024)(128)(4,1)} %bitcast.139), calls=%async_computation.8 | async-start | bytes 2097152
  106.5 7.9 %slice-start.1 = ((s8[9437184]{0:T(1024)(128)(4,1)}), s8[4194304]{0:T(1024)(128)(4,1)S(1)}, s32[]{:S(2)}) async-start(s8[9437184]{0:T(1024)(128)(4,1)} %bitcast.139), calls=%async_computation.9 | async-start | bytes 8388608
  106.5 7.9 %slice-start.2 = ((s8[9437184]{0:T(1024)(128)(4,1)}), s8[4194304]{0:T(1024)(128)(4,1)S(1)}, s32[]{:S(2)}) async-start(s8[9437184]{0:T(1024)(128)(4,1)} %bitcast.139), calls=%async_computation.10 | async-start | bytes 8388608
  114.4 19.7 %copy-start.8 = (f32[3072]{0:T(1024)S(1)}, f32[3072]{0:T(1024)}, u32[]{:S(2)}) copy-start(f32[3072]{0:T(1024)} %param.28) | copy-start | bytes 36868
  114.4 23.0 %copy-start.9 = (f32[3072]{0:T(1024)S(1)}, f32[3072]{0:T(1024)}, u32[]{:S(2)}) copy-start(f32[3072]{0:T(1024)} %param.29) | copy-start | bytes 36868
  114.4 23.0 %copy-start.10 = (f32[3072]{0:T(1024)S(1)}, f32[3072]{0:T(1024)}, u32[]{:S(2)}) copy-start(f32[3072]{0:T(1024)} %param.30) | copy-start | bytes 36868
  186.4 156.8 %reduce-scatter.11.cloned.1.call-start = ((), (), s32[]{:S(2)}) async-start(), calls=%async_computation.6 | async-start | bytes 10616832 | tf_op jit(solution)/shard_map/reduce_scatter | solution.py:167
  186.4 6.3 %copy-start = (f32[256,1536]{1,0:T(8,128)S(1)}, f32[256,1536]{1,0:T(8,128)}, u32[]{:S(2)}) copy-start(f32[256,1536]{1,0:T(8,128)} %get-tuple-element.62) | copy-start | bytes 4718596
  200.4 0.9 copy-start.2
  200.4 0.9 copy-start.4
  200.4 1.9 copy-start.3
Sparse Core Ops, SparseCore 0:
  60.6 20.6 reduce-scatter.6
  84.9 38.1 reduce-scatter.8
  186.5 76.4 reduce-scatter.12
  266.3 76.8 reduce-scatter.10
